TPU v7x, 32 devices: a whole 2x2x4 slice. The times are simulated.
32 devices in a mesh: batch: 8 (over y, x, core), rows: 4 (over z).
Axes of the slice: x: 2, y: 2, z: 4, core: 2. Of those that a mesh axis runs over, the one named last changes fastest.
Arguments:
- fine_level: bfloat16 [8, 32, 192, 384], P('batch', 'rows'), may hold values from -40 to 40
- middle_level: bfloat16 [8, 16, 96, 384], P('batch', 'rows'), may hold values from -40 to 40
- coarse_level: bfloat16 [8, 8, 48, 384], P('batch', 'rows'), may hold values from -40 to 40
- two_input_weights: float32 [2, 3, 2], replicated, may hold values from 0.5 to 2
- three_input_weights: float32 [2, 3], replicated, may hold values from 0.5 to 2
- depthwise: bfloat16 [2, 4, 3, 3, 384], replicated, may hold values from -2 to 2
- pointwise: bfloat16 [2, 4, 384, 384], replicated, may hold values from -0.3125 to 0.3125
- bn_gain: float32 [2, 4, 384], replicated, may hold values from 0.5 to 1.5
- bn_bias: float32 [2, 4, 384], replicated, may hold values from -3 to 3
Outputs:
- fine_result: bfloat16 [8, 32, 192, 384], P('batch', 'rows')
- middle_result: bfloat16 [8, 16, 96, 384], P('batch', 'rows')
- coarse_result: bfloat16 [8, 8, 48, 384], P('batch', 'rows')
All inputs are finite; a program needn't handle non-finite values.
Results may differ from a plain program's by a relative error of at most 0.025.
Values may be sent and summed in bfloat16 or wider, within the bound.
A program may use at most 64 MiB of HBM per device.

v0:
```python
import jax
import jax.numpy as jnp
from jax import lax
from jax.sharding import PartitionSpec as P

LAYERS = 2


def from_behind(block, axis, distance):
    devices = range(lax.axis_size(axis))
    route = [(i - distance, i) for i in devices if i - distance in devices]
    return lax.ppermute(block, axis, route)


def extended_2(block, sides, width):
    for axis, dim in sides:
        count = lax.axis_size(axis)
        forward = [(i, i + 1) for i in range(count - 1)]
        backward = [(target, source) for source, target in forward]
        low = lax.ppermute(
            lax.slice_in_dim(block, block.shape[dim] - width, None, axis=dim), axis, forward
        )
        high = lax.ppermute(lax.slice_in_dim(block, 0, width, axis=dim), axis, backward)
        block = jnp.concatenate([low, block, high], axis=dim)
    return block


def upsample(feature_maps):
    return jnp.repeat(jnp.repeat(feature_maps, 2, axis=1), 2, axis=2)


def reduce_resolution(feature_maps):
    beneath = from_behind(feature_maps[:, :1], "rows", -1)
    lowest = jnp.array(-jnp.inf, feature_maps.dtype)
    at_bottom = lax.axis_index("rows") == lax.axis_size("rows") - 1
    beneath = jnp.where(at_bottom, lowest, beneath)
    extended = jnp.concatenate([feature_maps, beneath], axis=1)
    padded = jnp.pad(extended, ((0, 0), (0, 0), (0, 1), (0, 0)), constant_values=lowest)
    return lax.reduce_window(padded, lowest, lax.max, (1, 3, 3, 1), (1, 2, 2, 1), "VALID")


def weighted_join_activate(inputs_list, weights):
    weight_sum = jnp.sum(weights) + 0.0001
    running = weights[0] * inputs_list[0].astype(jnp.float32)
    for position in range(1, len(inputs_list)):
        running = running + weights[position] * inputs_list[position].astype(jnp.float32)
    return jax.nn.silu(running / weight_sum).astype(jnp.bfloat16)


def separable(extended, kernel, projection):
    padded = jnp.pad(extended, ((0, 0), (0, 0), (1, 1), (0, 0)))
    height = extended.shape[1] - 2
    width = extended.shape[2]
    running = jnp.zeros((extended.shape[0], height, width, extended.shape[3]), jnp.float32)
    for row_tap in range(3):
        for col_tap in range(3):
            window = padded[:, row_tap : row_tap + height, col_tap : col_tap + width, :]
            running = running + window.astype(jnp.float32) * kernel[row_tap, col_tap].astype(
                jnp.float32
            )
    spatial = running.astype(jnp.bfloat16)
    projected = jnp.dot(
        spatial.reshape(-1, spatial.shape[-1]), projection, preferred_element_type=jnp.float32
    )
    return projected.reshape(spatial.shape)


def normalize(projected, gain, offset):
    count = float(
        projected.shape[0]
        * projected.shape[1]
        * projected.shape[2]
        * lax.axis_size("batch")
        * lax.axis_size("rows")
    )
    totals, squares = lax.psum(
        (jnp.sum(projected, axis=(0, 1, 2)), jnp.sum(projected * projected, axis=(0, 1, 2))),
        ("batch", "rows"),
    )
    center = totals / count
    spread = squares / count - center * center
    centered = projected - center
    return (centered * lax.rsqrt(spread + 1e-05) * gain + offset).astype(jnp.bfloat16)


def node(activated, kernel, projection, gain, offset):
    extended = extended_2(activated, (("rows", 1),), 1)
    return normalize(separable(extended, kernel, projection), gain, offset)


def body(
    fine_level,
    middle_level,
    coarse_level,
    two_input_weights,
    three_input_weights,
    depthwise,
    pointwise,
    bn_gain,
    bn_bias,
):
    fine, middle_grid, coarse_grid = (fine_level, middle_level, coarse_level)
    for bidirectional_layer in range(LAYERS):

        def run_layer_pair(index, activated):
            return node(
                activated,
                depthwise[bidirectional_layer, index],
                pointwise[bidirectional_layer, index],
                bn_gain[bidirectional_layer, index],
                bn_bias[bidirectional_layer, index],
            )

        downward_middle = run_layer_pair(
            0,
            weighted_join_activate(
                [middle_grid, upsample(coarse_grid)], two_input_weights[bidirectional_layer, 0]
            ),
        )
        updated_fine = run_layer_pair(
            1,
            weighted_join_activate(
                [fine, upsample(downward_middle)], two_input_weights[bidirectional_layer, 1]
            ),
        )
        updated_middle = run_layer_pair(
            2,
            weighted_join_activate(
                [middle_grid, downward_middle, reduce_resolution(updated_fine)],
                three_input_weights[bidirectional_layer],
            ),
        )
        updated_coarse = run_layer_pair(
            3,
            weighted_join_activate(
                [coarse_grid, reduce_resolution(updated_middle)],
                two_input_weights[bidirectional_layer, 2],
            ),
        )
        fine, middle_grid, coarse_grid = (updated_fine, updated_middle, updated_coarse)
    return (fine, middle_grid, coarse_grid)


def solution(mesh):
    in_specs = (
        P("batch", "rows", None, None),
        P("batch", "rows", None, None),
        P("batch", "rows", None, None),
        P(),
        P(),
        P(),
        P(),
        P(),
        P(),
    )
    out_specs = (
        P("batch", "rows", None, None),
        P("batch", "rows", None, None),
        P("batch", "rows", None, None),
    )
    return jax.shard_map(body, mesh=mesh, in_specs=in_specs, out_specs=out_specs, check_vma=False)
```

profile of v0, /device:TPU:0, one launch (start us, length us, event | category | flops | bytes accessed | tf_op | source)
XLA Modules:
  0.0 496.3 jit_solution(17493123043353743994)
XLA Ops:
  7.4 5.0 collective-permute-start
  20.6 40.4 %all-reduce.15 = (f32[384]{0:T(512)S(1)}, f32[384]{0:T(512)S(1)}) all-reduce(f32[384]{0:T(512)S(1)} %get-tuple-element.14, f32[384]{0:T(512)S(1)} %get-tuple-element.13), channel_id=1, replica_groups=mesh['batch'=8,'rows'=4] {'batch','rows'}, use_global_device_ids=true, to_apply=%region_4.5 | all-reduce | flops 768 | bytes 6144 | tf_op jit(solution)/shard_map/psum | solution.py:76
  64.7 3.2 mul.1426
  74.4 4.4 collective-permute-done.3
  79.2 2.4 add_convert_fusion.3
  83.5 40.1 %all-reduce.14 = (f32[384]{0:T(512)S(1)}, f32[384]{0:T(512)S(1)}) all-reduce(f32[384]{0:T(512)S(1)} %get-tuple-element.6, f32[384]{0:T(512)S(1)} %get-tuple-element.5), channel_id=1, replica_groups=mesh['batch'=8,'rows'=4] {'batch','rows'}, use_global_device_ids=true, to_apply=%region_9.10 | all-reduce | flops 768 | bytes 6144 | tf_op jit(solution)/shard_map/psum | solution.py:76
  137.6 3.4 multiply_convert_fusion.4
  141.0 2.4 collective-permute-start.5
  145.4 4.3 collective-permute-done.6
  151.8 40.2 %all-reduce.13 = (f32[384]{0:T(512)S(1)}, f32[384]{0:T(512)S(1)}) all-reduce(f32[384]{0:T(512)S(1)} %get-tuple-element.12, f32[384]{0:T(512)S(1)} %get-tuple-element.11), channel_id=1, replica_groups=mesh['batch'=8,'rows'=4] {'batch','rows'}, use_global_device_ids=true, to_apply=%region_15.16 | all-reduce | flops 768 | bytes 6144 | tf_op jit(solution)/shard_map/psum | solution.py:76
  194.7 3.7 collective-permute-done.7
  201.8 3.1 collective-permute-start.8
  207.5 3.2 collective-permute-done.9
  212.1 39.2 %all-reduce.12 = (f32[384]{0:T(512)S(1)}, f32[384]{0:T(512)S(1)}) all-reduce(f32[384]{0:T(512)S(1)} %get-tuple-element.18, f32[384]{0:T(512)S(1)} %get-tuple-element.17), channel_id=1, replica_groups=mesh['batch'=8,'rows'=4] {'batch','rows'}, use_global_device_ids=true, to_apply=%region_21.22 | all-reduce | flops 768 | bytes 6144 | tf_op jit(solution)/shard_map/psum | solution.py:76
  256.2 3.3 collective-permute-start.10
  261.4 4.3 collective-permute-done.11
  267.7 40.0 %all-reduce.11 = (f32[384]{0:T(512)S(1)}, f32[384]{0:T(512)S(1)}) all-reduce(f32[384]{0:T(512)S(1)} %get-tuple-element.10, f32[384]{0:T(512)S(1)} %get-tuple-element.9), channel_id=1, replica_groups=mesh['batch'=8,'rows'=4] {'batch','rows'}, use_global_device_ids=true, to_apply=%region_26.27 | all-reduce | flops 768 | bytes 6144 | tf_op jit(solution)/shard_map/psum | solution.py:76
  311.3 4.1 mul.1555
  315.4 3.3 multiply_convert_fusion
  318.7 3.3 collective-permute-start.12
  324.7 4.4 collective-permute-done.13
  329.5 2.4 add_convert_fusion.1
  333.8 39.1 %all-reduce.10 = (f32[384]{0:T(512)S(1)}, f32[384]{0:T(512)S(1)}) all-reduce(f32[384]{0:T(512)S(1)} %get-tuple-element.4, f32[384]{0:T(512)S(1)} %get-tuple-element.3), channel_id=1, replica_groups=mesh['batch'=8,'rows'=4] {'batch','rows'}, use_global_device_ids=true, to_apply=%region_31.32 | all-reduce | flops 768 | bytes 6144 | tf_op jit(solution)/shard_map/psum | solution.py:76
  376.3 5.0 %collective-permute-done.14 = bf16[1,1,192,384]{3,2,1,0:T(8,128)(2,1)S(1)} collective-permute-done((bf16[1,1,192,384]{3,2,1,0:T(8,128)(2,1)S(1)}, bf16[1,1,192,384]{3,2,1,0:T(8,128)(2,1)S(1)}, u32[]{:S(2)}, u32[]{:S(2)}) %collective-permute-start.14) | collective-permute-done | bytes 147488 | tf_op jit(solution)/shard_map/ppermute | solution.py:12
  382.8 3.4 multiply_convert_fusion.2
  386.2 3.3 collective-permute-start.15
  391.5 4.3 collective-permute-done.16
  397.8 40.1 %all-reduce.9 = (f32[384]{0:T(512)S(1)}, f32[384]{0:T(512)S(1)}) all-reduce(f32[384]{0:T(512)S(1)} %get-tuple-element.8, f32[384]{0:T(512)S(1)} %get-tuple-element.7), channel_id=1, replica_groups=mesh['batch'=8,'rows'=4] {'batch','rows'}, use_global_device_ids=true, to_apply=%region_37.38 | all-reduce | flops 768 | bytes 6144 | tf_op jit(solution)/shard_map/psum | solution.py:76
  440.1 4.3 collective-permute-done.17
  446.0 3.3 collective-permute-start.18
  451.0 4.2 collective-permute-done.19
  456.6 39.0 %all-reduce.8 = (f32[384]{0:T(512)S(1)}, f32[384]{0:T(512)S(1)}) all-reduce(f32[384]{0:T(512)S(1)} %get-tuple-element.16, f32[384]{0:T(512)S(1)} %get-tuple-element.15), channel_id=1, replica_groups=mesh['batch'=8,'rows'=4] {'batch','rows'}, use_global_device_ids=true, to_apply=%region_43.44 | all-reduce | flops 768 | bytes 6144 | tf_op jit(solution)/shard_map/psum | solution.py:76
  (235 shorter events, 83.1 us)
Async XLA Ops:
  7.4 9.0 %collective-permute-start = (bf16[1,1,96,384]{3,2,1,0:T(8,128)(2,1)S(1)}, bf16[1,1,96,384]{3,2,1,0:T(8,128)(2,1)S(1)}, u32[]{:S(2)}, u32[]{:S(2)}) collective-permute-start(bf16[1,1,96,384]{3,2,1,0:T(8,128)(2,1)S(1)} %get-tuple-element.141), channel_id=1, source_target_pairs={{0,1},{1,2},{2,3},{4,5},{5,6},{6,7},{8,9},{9,10},{10,11},{12,13},{... | collective-permute-start | bytes 221192 | tf_op jit(solution)/shard_map/ppermute | solution.py:20
  12.4 6.2 %collective-permute-start.1 = (bf16[1,1,96,384]{3,2,1,0:T(8,128)(2,1)S(1)}, bf16[1,1,96,384]{3,2,1,0:T(8,128)(2,1)S(1)}, u32[]{:S(2)}, u32[]{:S(2)}) collective-permute-start(bf16[1,1,96,384]{3,2,1,0:T(8,128)(2,1)S(1)} %get-tuple-element.142), channel_id=1, source_target_pairs={{1,0},{2,1},{3,2},{5,4},{6,5},{7,6},{9,8},{10,9},{11,10},{13,12},{... | collective-permute-start | bytes 221192 | tf_op jit(solution)/shard_map/ppermute | solution.py:23
  16.4 238.2 %copy-start.21 = (f32[384]{0:T(512)}, f32[384]{0:T(512)S(1)}, u32[]{:S(2)}) copy-start(f32[384]{0:T(512)S(1)} %get-tuple-element.31) | copy-start | bytes 4612
  69.4 5.0 %collective-permute-start.2 = (bf16[1,1,192,384]{3,2,1,0:T(8,128)(2,1)S(1)}, bf16[1,1,192,384]{3,2,1,0:T(8,128)(2,1)S(1)}, u32[]{:S(2)}, u32[]{:S(2)}) collective-permute-start(bf16[1,1,192,384]{3,2,1,0:T(8,128)(2,1)S(1)} %get-tuple-element.133), channel_id=1, source_target_pairs={{0,1},{1,2},{2,3},{4,5},{5,6},{6,7},{8,9},{9,10},{10,11},{12,13},{... | collective-permute-start | bytes 442376 | tf_op jit(solution)/shard_map/ppermute | solution.py:20
  71.7 7.0 %collective-permute-start.3 = (bf16[1,1,192,384]{3,2,1,0:T(8,128)(2,1)S(1)}, bf16[1,1,192,384]{3,2,1,0:T(8,128)(2,1)S(1)}, u32[]{:S(2)}, u32[]{:S(2)}) collective-permute-start(bf16[1,1,192,384]{3,2,1,0:T(8,128)(2,1)S(1)} %get-tuple-element.134), channel_id=1, source_target_pairs={{1,0},{2,1},{3,2},{5,4},{6,5},{7,6},{9,8},{10,9},{11,10},{13,12},{... | collective-permute-start | bytes 442376 | tf_op jit(solution)/shard_map/ppermute | solution.py:23
  125.9 7.3 %collective-permute-start.4 = (bf16[1,1,192,384]{3,2,1,0:T(8,128)(2,1)}, bf16[1,1,192,384]{3,2,1,0:T(8,128)(2,1)}, u32[]{:S(2)}, u32[]{:S(2)}) collective-permute-start(bf16[1,1,192,384]{3,2,1,0:T(8,128)(2,1)} %slice.974), channel_id=1, source_target_pairs={{1,0},{2,1},{3,2},{5,4},{6,5},{7,6},{9,8},{10,9},{11,10},{13,12},{... | collective-permute-start | bytes 442376 | tf_op jit(solution)/shard_map/ppermute | solution.py:12
  141.0 4.4 collective-permute-start.5
  143.5 48.5 %copy-start.23 = (f32[384]{0:T(512)S(1)}, f32[384]{0:T(512)}, u32[]{:S(2)}) copy-start(f32[384]{0:T(512)} %get-tuple-element.208) | copy-start | bytes 4612
  143.5 6.2 %collective-permute-start.6 = (bf16[1,1,96,384]{3,2,1,0:T(8,128)(2,1)S(1)}, bf16[1,1,96,384]{3,2,1,0:T(8,128)(2,1)S(1)}, u32[]{:S(2)}, u32[]{:S(2)}) collective-permute-start(bf16[1,1,96,384]{3,2,1,0:T(8,128)(2,1)S(1)} %get-tuple-element.140), channel_id=1, source_target_pairs={{1,0},{2,1},{3,2},{5,4},{6,5},{7,6},{9,8},{10,9},{11,10},{13,12},{... | collective-permute-start | bytes 221192 | tf_op jit(solution)/shard_map/ppermute | solution.py:23
  150.4 50.0 %copy-start.10 = (bf16[1,2,48,384]{3,2,1,0:T(8,128)(2,1)S(1)}, bf16[1,2,48,384]{3,2,1,0:T(8,128)(2,1)}, u32[]{:S(2)}) copy-start(bf16[1,2,48,384]{3,2,1,0:T(8,128)(2,1)} %param.11) | copy-start | bytes 221188
  151.7 102.8 %copy-start.1 = (f32[384,384]{1,0:T(8,128)}, f32[384,384]{1,0:T(8,128)S(1)}, u32[]{:S(2)}) copy-start(f32[384,384]{1,0:T(8,128)S(1)} %get-tuple-element.191) | copy-start | bytes 1769476
  151.7 99.6 %copy-start.32 = (f32[384]{0:T(512)S(1)}, f32[384]{0:T(512)}, u32[]{:S(2)}) copy-start(f32[384]{0:T(512)} %get-tuple-element.30) | copy-start | bytes 4612
  151.8 99.6 %copy-start.34 = (f32[384]{0:T(512)S(1)}, f32[384]{0:T(512)}, u32[]{:S(2)}) copy-start(f32[384]{0:T(512)} %get-tuple-element.209) | copy-start | bytes 4612
  192.0 60.0 %copy-start.25 = (f32[384]{0:T(512)}, f32[384]{0:T(512)S(1)}, u32[]{:S(2)}) copy-start(f32[384]{0:T(512)S(1)} %get-tuple-element.177) | copy-start | bytes 4612
  192.0 60.0 %copy-start.27 = (f32[384]{0:T(512)}, f32[384]{0:T(512)S(1)}, u32[]{:S(2)}) copy-start(f32[384]{0:T(512)S(1)} %get-tuple-element.178) | copy-start | bytes 4612
  192.1 6.2 %collective-permute-start.7 = (bf16[1,1,96,384]{3,2,1,0:T(8,128)(2,1)S(1)}, bf16[1,1,96,384]{3,2,1,0:T(8,128)(2,1)S(1)}, u32[]{:S(2)}, u32[]{:S(2)}) collective-permute-start(bf16[1,1,96,384]{3,2,1,0:T(8,128)(2,1)S(1)} %slice.992), channel_id=1, source_target_pairs={{1,0},{2,1},{3,2},{5,4},{6,5},{7,6},{9,8},{10,9},{11,10},{13,12},{... | collective-permute-start | bytes 221192 | tf_op jit(solution)/shard_map/ppermute | solution.py:12
  201.8 5.7 %collective-permute-start.8 = (bf16[1,1,48,384]{3,2,1,0:T(8,128)(2,1)S(1)}, bf16[1,1,48,384]{3,2,1,0:T(8,128)(2,1)S(1)}, u32[]{:S(2)}, u32[]{:S(2)}) collective-permute-start(bf16[1,1,48,384]{3,2,1,0:T(8,128)(2,1)S(1)} %get-tuple-element.145), channel_id=1, source_target_pairs={{0,1},{1,2},{2,3},{4,5},{5,6},{6,7},{8,9},{9,10},{10,11},{12,13},{... | collective-permute-start | bytes 110600 | tf_op jit(solution)/shard_map/ppermute | solution.py:20
  204.9 5.9 %collective-permute-start.9 = (bf16[1,1,48,384]{3,2,1,0:T(8,128)(2,1)S(1)}, bf16[1,1,48,384]{3,2,1,0:T(8,128)(2,1)S(1)}, u32[]{:S(2)}, u32[]{:S(2)}) collective-permute-start(bf16[1,1,48,384]{3,2,1,0:T(8,128)(2,1)S(1)} %get-tuple-element.146), channel_id=1, source_target_pairs={{1,0},{2,1},{3,2},{5,4},{6,5},{7,6},{9,8},{10,9},{11,10},{13,12},{... | collective-permute-start | bytes 110600 | tf_op jit(solution)/shard_map/ppermute | solution.py:23
  212.1 48.7 %copy-start.14 = (bf16[3,3,384]{2,1,0:T(4,128)(2,1)S(1)}, bf16[3,3,384]{2,1,0:T(4,128)(2,1)}, u32[]{:S(2)}) copy-start(bf16[3,3,384]{2,1,0:T(4,128)(2,1)} %get-tuple-element.200) | copy-start | bytes 20740
  256.2 5.3 %collective-permute-start.10 = (bf16[1,1,96,384]{3,2,1,0:T(8,128)(2,1)S(1)}, bf16[1,1,96,384]{3,2,1,0:T(8,128)(2,1)S(1)}, u32[]{:S(2)}, u32[]{:S(2)}) collective-permute-start(bf16[1,1,96,384]{3,2,1,0:T(8,128)(2,1)S(1)} %get-tuple-element.137), channel_id=1, source_target_pairs={{0,1},{1,2},{2,3},{4,5},{5,6},{6,7},{8,9},{9,10},{10,11},{12,13},{... | collective-permute-start | bytes 221192 | tf_op jit(solution)/shard_map/ppermute | solution.py:20
  259.5 6.2 %collective-permute-start.11 = (bf16[1,1,96,384]{3,2,1,0:T(8,128)(2,1)S(1)}, bf16[1,1,96,384]{3,2,1,0:T(8,128)(2,1)S(1)}, u32[]{:S(2)}, u32[]{:S(2)}) collective-permute-start(bf16[1,1,96,384]{3,2,1,0:T(8,128)(2,1)S(1)} %get-tuple-element.138), channel_id=1, source_target_pairs={{1,0},{2,1},{3,2},{5,4},{6,5},{7,6},{9,8},{10,9},{11,10},{13,12},{... | collective-permute-start | bytes 221192 | tf_op jit(solution)/shard_map/ppermute | solution.py:23
  318.7 6.0 %collective-permute-start.12 = (bf16[1,1,192,384]{3,2,1,0:T(8,128)(2,1)S(1)}, bf16[1,1,192,384]{3,2,1,0:T(8,128)(2,1)S(1)}, u32[]{:S(2)}, u32[]{:S(2)}) collective-permute-start(bf16[1,1,192,384]{3,2,1,0:T(8,128)(2,1)S(1)} %get-tuple-element.131), channel_id=1, source_target_pairs={{0,1},{1,2},{2,3},{4,5},{5,6},{6,7},{8,9},{9,10},{10,11},{12,13},{... | collective-permute-start | bytes 442376 | tf_op jit(solution)/shard_map/ppermute | solution.py:20
  322.1 7.0 %collective-permute-start.13 = (bf16[1,1,192,384]{3,2,1,0:T(8,128)(2,1)S(1)}, bf16[1,1,192,384]{3,2,1,0:T(8,128)(2,1)S(1)}, u32[]{:S(2)}, u32[]{:S(2)}) collective-permute-start(bf16[1,1,192,384]{3,2,1,0:T(8,128)(2,1)S(1)} %get-tuple-element.132), channel_id=1, source_target_pairs={{1,0},{2,1},{3,2},{5,4},{6,5},{7,6},{9,8},{10,9},{11,10},{13,12},{... | collective-permute-start | bytes 442376 | tf_op jit(solution)/shard_map/ppermute | solution.py:23
  374.1 7.2 %collective-permute-start.14 = (bf16[1,1,192,384]{3,2,1,0:T(8,128)(2,1)S(1)}, bf16[1,1,192,384]{3,2,1,0:T(8,128)(2,1)S(1)}, u32[]{:S(2)}, u32[]{:S(2)}) collective-permute-start(bf16[1,1,192,384]{3,2,1,0:T(8,128)(2,1)S(1)} %slice.1044), channel_id=1, source_target_pairs={{1,0},{2,1},{3,2},{5,4},{6,5},{7,6},{9,8},{10,9},{11,10},{13,12},{... | collective-permute-start | bytes 442376 | tf_op jit(solution)/shard_map/ppermute | solution.py:12
  386.2 5.3 %collective-permute-start.15 = (bf16[1,1,96,384]{3,2,1,0:T(8,128)(2,1)S(1)}, bf16[1,1,96,384]{3,2,1,0:T(8,128)(2,1)S(1)}, u32[]{:S(2)}, u32[]{:S(2)}) collective-permute-start(bf16[1,1,96,384]{3,2,1,0:T(8,128)(2,1)S(1)} %get-tuple-element.135), channel_id=1, source_target_pairs={{0,1},{1,2},{2,3},{4,5},{5,6},{6,7},{8,9},{9,10},{10,11},{12,13},{... | collective-permute-start | bytes 221192 | tf_op jit(solution)/shard_map/ppermute | solution.py:20
  389.6 6.2 %collective-permute-start.16 = (bf16[1,1,96,384]{3,2,1,0:T(8,128)(2,1)S(1)}, bf16[1,1,96,384]{3,2,1,0:T(8,128)(2,1)S(1)}, u32[]{:S(2)}, u32[]{:S(2)}) collective-permute-start(bf16[1,1,96,384]{3,2,1,0:T(8,128)(2,1)S(1)} %get-tuple-element.136), channel_id=1, source_target_pairs={{1,0},{2,1},{3,2},{5,4},{6,5},{7,6},{9,8},{10,9},{11,10},{13,12},{... | collective-permute-start | bytes 221192 | tf_op jit(solution)/shard_map/ppermute | solution.py:23
  397.8 97.8 %copy-start.54 = (f32[384]{0:T(512)S(1)}, f32[384]{0:T(512)}, u32[]{:S(2)}) copy-start(f32[384]{0:T(512)} %get-tuple-element.27) | copy-start | bytes 4612
  397.8 97.8 %copy-start.55 = (f32[384]{0:T(512)S(1)}, f32[384]{0:T(512)}, u32[]{:S(2)}) copy-start(f32[384]{0:T(512)} %get-tuple-element.212) | copy-start | bytes 4612
  438.1 58.2 %copy-start.5 = (bf16[1,4,96,384]{3,2,1,0:T(8,128)(2,1)}, bf16[1,4,96,384]{3,2,1,0:T(8,128)(2,1)S(1)}, u32[]{:S(2)}) copy-start(bf16[1,4,96,384]{3,2,1,0:T(8,128)(2,1)S(1)} %add_convert_fusion.4) | copy-start | bytes 884740
  438.1 6.2 %collective-permute-start.17 = (bf16[1,1,96,384]{3,2,1,0:T(8,128)(2,1)S(1)}, bf16[1,1,96,384]{3,2,1,0:T(8,128)(2,1)S(1)}, u32[]{:S(2)}, u32[]{:S(2)}) collective-permute-start(bf16[1,1,96,384]{3,2,1,0:T(8,128)(2,1)S(1)} %slice.1062), channel_id=1, source_target_pairs={{1,0},{2,1},{3,2},{5,4},{6,5},{7,6},{9,8},{10,9},{11,10},{13,12},{... | collective-permute-start | bytes 221192 | tf_op jit(solution)/shard_map/ppermute | solution.py:12
  446.0 5.0 %collective-permute-start.18 = (bf16[1,1,48,384]{3,2,1,0:T(8,128)(2,1)S(1)}, bf16[1,1,48,384]{3,2,1,0:T(8,128)(2,1)S(1)}, u32[]{:S(2)}, u32[]{:S(2)}) collective-permute-start(bf16[1,1,48,384]{3,2,1,0:T(8,128)(2,1)S(1)} %get-tuple-element.143), channel_id=1, source_target_pairs={{0,1},{1,2},{2,3},{4,5},{5,6},{6,7},{8,9},{9,10},{10,11},{12,13},{... | collective-permute-start | bytes 110600 | tf_op jit(solution)/shard_map/ppermute | solution.py:20
  449.4 5.9 %collective-permute-start.19 = (bf16[1,1,48,384]{3,2,1,0:T(8,128)(2,1)S(1)}, bf16[1,1,48,384]{3,2,1,0:T(8,128)(2,1)S(1)}, u32[]{:S(2)}, u32[]{:S(2)}) collective-permute-start(bf16[1,1,48,384]{3,2,1,0:T(8,128)(2,1)S(1)} %get-tuple-element.144), channel_id=1, source_target_pairs={{1,0},{2,1},{3,2},{5,4},{6,5},{7,6},{9,8},{10,9},{11,10},{13,12},{... | collective-permute-start | bytes 110600 | tf_op jit(solution)/shard_map/ppermute | solution.py:23
  (46 other events, 960.3 us)
where the time goes:
time: 499 us; the launch traced here: 496 us
  blocking collectives  318 us (64%)
  waiting for transfers between devices  49.7 us (10%)
  other arithmetic  43 us (9%)
  starting transfers between devices  42.1 us (8%)
  local copies, waits for them, and re-layouts  24.9 us (5%)
  matrix products  11.5 us (2%)
  between operations  6.92 us (1%)
    psum x8, blocking collectives, normalize(): lax.psum((jnp.sum(projected, axis=(0, 1, 2)), jnp.sum(projected * project...  318 us
    ppermute x8, waiting for transfers between devices, extended_2(): lax.ppermute(lax.slice_in_dim(block, 0, width, axis=dim), axis, backward)  31.3 us
    ppermute x8, starting transfers between devices, extended_2(): lax.ppermute(lax.slice_in_dim(block, block.shape[dim] - width, None, axis...  26.1 us
    convert_element_type x8, other arithmetic, weighted_join_activate(): return jax.nn.silu(running / weight_sum).astype(jnp.bfloat16)  16.5 us
    ppermute x4, waiting for transfers between devices, from_behind(): return lax.ppermute(block, axis, route)  15.3 us
    dot_general x8, matrix products, separable(): jnp.dot(spatial.reshape(-1, spatial.shape[-1]), projection, preferred_ele...  11.5 us
    ppermute x8, starting transfers between devices, extended_2(): lax.ppermute(lax.slice_in_dim(block, 0, width, axis=dim), axis, backward)  10.7 us
  transfers between devices with their start and end apart: 20, of which 18 were waited for; matrix products, arithmetic and copies ran while one was open for 1% of the time, Pallas kernels for 0%

commit v1 on v0

v1 whole, which is shorter than its diff:
```python
import functools

import jax
import jax.numpy as jnp
from jax import lax
from jax.experimental import pallas as pl
from jax.experimental.pallas import tpu as pltpu
from jax.sharding import PartitionSpec as P

LAYERS = 2
NODES = 4
MESH = pl.DeviceIdType.MESH
F32 = jnp.float32
BF16 = jnp.bfloat16
PAD = 8


def permutation(size, phases, inverse):
    part = size // phases
    natural = lax.broadcasted_iota(jnp.int32, (size, size), 0 if inverse else 1)
    ordered = lax.broadcasted_iota(jnp.int32, (size, size), 1 if inverse else 0)
    phase = jnp.zeros((size, size), jnp.int32)
    for p in range(1, phases):
        phase = phase + jnp.where(ordered >= p * part, 1, 0)
    hit = natural == phases * (ordered - phase * part) + phase
    return jnp.where(hit, 1.0, 0.0).astype(BF16)


def rounded(x):
    return x.astype(BF16).astype(F32)


def kernel(
    nb, nr,
    fine, mid, top, w2, w3, dw, pw_in, gain, bias,
    out_f, out_m, out_t,
    afine, amid, atop, pw, act, sp, raw_f, raw_d, raw_m, raw_t,
    cpf, cpm, pool_f, pool_m, nf, nm, nt,
    up_f, dn_f, up_m, dn_m, rup_f, rdn_f, rup_m, rdn_m, rup_t, rdn_t,
    perm_f, perm_m, stat_b, stat_r, of_v, om_v, ot_v,
    sb_s, sb_r, sr_s, sr_r, h_s, h_r, loc, outs,
):
    b_me = lax.axis_index("batch")
    r_me = lax.axis_index("rows")
    has_up = r_me > 0
    has_dn = r_me < nr - 1
    above = jnp.maximum(r_me - 1, 0)
    below = jnp.minimum(r_me + 1, nr - 1)
    Rf, Wf, C = fine.shape[1:]
    Rm, Wm = mid.shape[1:3]
    Rt, J = top.shape[1:3]
    Pf, Pm = Wf // J, Wm // J
    images = nb * fine.shape[0]

    loads = [
        pltpu.make_async_copy(mid.at[0], amid.at[pl.ds(2, Rm)], loc.at[0]),
        pltpu.make_async_copy(top.at[0], atop.at[pl.ds(1, Rt)], loc.at[1]),
        pltpu.make_async_copy(pw_in, pw, loc.at[2]),
        pltpu.make_async_copy(fine.at[0], afine.at[pl.ds(1, Rf)], loc.at[3]),
    ]
    for copy in loads:
        copy.start()

    barrier = pltpu.get_barrier_semaphore()
    for d in range(1, nb):
        pl.semaphore_signal(
            barrier, inc=1, device_id={"batch": lax.rem(b_me + d, nb)}, device_id_type=MESH
        )
    for d in range(1, nr):
        pl.semaphore_signal(
            barrier, inc=1, device_id={"rows": lax.rem(r_me + d, nr)}, device_id_type=MESH
        )

    def message(k, src, dst, up):
        return pltpu.make_async_remote_copy(
            src_ref=src, dst_ref=dst, send_sem=h_s.at[k], recv_sem=h_r.at[k],
            device_id={"rows": above if up else below}, device_id_type=MESH,
        )

    def send(k, src, dst, up):
        @pl.when(has_up if up else has_dn)
        def _():
            message(k, src, dst, up).start()

    def arrive(k, src, dst, up):
        @pl.when(has_dn if up else has_up)
        def _():
            message(k, src, dst, up).wait_recv()

        @pl.when(has_up if up else has_dn)
        def _():
            message(k, src, dst, up).wait_send()

    def spread_copies(store, sends, recvs, node, me, count, axis):
        return [
            pltpu.make_async_remote_copy(
                src_ref=store.at[node, me], dst_ref=store.at[node, me],
                send_sem=sends.at[node, d], recv_sem=recvs.at[node, d],
                device_id={axis: lax.rem(me + d, count)}, device_id_type=MESH,
            )
            for d in range(1, count)
        ]

    def stats_begin(node, total, square):
        stat_b[node, b_me, 0:1, :] = total
        stat_b[node, b_me, 1:2, :] = square
        copies = spread_copies(stat_b, sb_s, sb_r, node, b_me, nb, "batch")
        for copy in copies:
            copy.start()
        return copies

    def stats_middle(node, copies):
        for copy in copies:
            copy.wait_recv()
        stat_r[node, r_me] = jnp.sum(stat_b[node], axis=0)
        second = spread_copies(stat_r, sr_s, sr_r, node, r_me, nr, "rows")
        for copy in second:
            copy.start()
        for copy in copies:
            copy.wait_send()
        return second

    def stats_end(node, copies, layer, which, count):
        for copy in copies:
            copy.wait_recv()
        sums = jnp.sum(stat_r[node], axis=0)
        for copy in copies:
            copy.wait_send()
        center = sums[0:1] / count
        spread = sums[1:2] / count - center * center
        scale = lax.rsqrt(spread + 1e-05) * gain[layer, which : which + 1, :]
        return center, scale, bias[layer, which : which + 1, :]

    def normal(x, stats):
        center, scale, shift = stats
        return (x - center) * scale + shift

    def coefficients(weights):
        total = weights[0]
        for w in weights[1:]:
            total = total + w
        inverse = 0.5 / jnp.full((1, C), total + 0.0001, F32)
        return [jnp.full((1, C), w, F32) * inverse for w in weights]

    def activate(row, p, half, valid):
        a = rounded(half + half * jnp.tanh(half))
        act[row, p, pl.ds(PAD, J), :] = jnp.where(valid, a, 0.0)

    def depthwise(layer, which, rows, phases):
        taps = []
        for i in range(3):
            k = dw[layer, which, i].astype(F32)
            taps.append([k[j : j + 1] for j in range(3)])

        def body(r, carry):
            for p in range(phases):
                total = None
                for i in range(3):
                    for j in range(3):
                        q, at = p + j - 1, PAD
                        if q < 0:
                            q, at = phases - 1, PAD - 1
                        elif q >= phases:
                            q, at = 0, PAD + 1
                        term = act[r + i, q, pl.ds(at, J), :] * taps[i][j]
                        total = term if total is None else total + term
                sp[pl.ds(pl.multiple_of((r * phases + p) * J, J), J), :] = total.astype(BF16)
            return carry

        lax.fori_loop(0, rows, body, 0)

    def pointwise(layer, which, rows, phases, chunk, dst, skip):
        width = phases * J

        def one(first, carry):
            y = jnp.dot(
                sp[pl.ds(pl.multiple_of(first * width, J), chunk * width), :],
                pw[layer, which], preferred_element_type=F32,
            )
            for r in range(chunk):
                for p in range(phases):
                    a = (r * phases + p) * J
                    dst[first + r, p, pl.ds(0, J), :] = y[a : a + J]
            kept = y[skip * width : (chunk - skip) * width]
            return (
                carry[0] + jnp.sum(kept, axis=0, keepdims=True),
                carry[1] + jnp.sum(kept * kept, axis=0, keepdims=True),
            )

        zero = jnp.zeros((1, C), F32)
        if chunk == rows:
            return one(0, (zero, zero))
        return lax.fori_loop(0, rows // chunk, lambda i, c: one(i * chunk, c), (zero, zero))

    def column_pool(src, row, q, phases):
        a = jnp.maximum(src[row, 2 * q, pl.ds(0, J), :], src[row, 2 * q + 1, pl.ds(0, J), :])
        if 2 * q + 2 < phases:
            return jnp.maximum(a, src[row, 2 * q + 2, pl.ds(0, J), :])
        return jnp.maximum(a, src[row, 0, pl.ds(1, J), :])

    act[:, :, 0:PAD, :] = jnp.zeros((Rf + 2, Pf, PAD, C), F32)
    act[:, :, J + PAD : J + 2 * PAD, :] = jnp.zeros((Rf + 2, Pf, PAD, C), F32)
    raw_f[:, :, J : J + PAD, :] = jnp.full((Rf, Pf, PAD, C), -jnp.inf, F32)
    raw_m[:, :, J : J + PAD, :] = jnp.full((Rm, Pm, PAD, C), -jnp.inf, F32)

    pl.semaphore_wait(barrier, nb + nr - 2)
    first = [
        (0, mid.at[0, pl.ds(0, 2)], amid.at[pl.ds(Rm + 2, 2)], True),
        (1, mid.at[0, pl.ds(Rm - 2, 2)], amid.at[pl.ds(0, 2)], False),
        (2, top.at[0, 0], atop.at[Rt + 1], True),
        (3, top.at[0, Rt - 1], atop.at[0], False),
        (4, fine.at[0, 0], afine.at[Rf + 1], True),
        (5, fine.at[0, Rf - 1], afine.at[0], False),
    ]
    for m in first:
        send(*m)
    perm_f[0] = permutation(Wf, Pf, False)
    perm_f[1] = permutation(Wf, Pf, True)
    perm_m[0] = permutation(Wm, Pm, False)
    perm_m[1] = permutation(Wm, Pm, True)
    for copy in loads[:2]:
        copy.wait()
    for m in first[:4]:
        arrive(*m)

    def order_mid(e, carry):
        y = jnp.dot(perm_m[0], amid[e], preferred_element_type=F32).astype(BF16)
        for p in range(Pm):
            nm[0, e, p] = y[p * J : (p + 1) * J]
        return carry

    lax.fori_loop(0, Rm + 4, order_mid, 0)
    nt[0] = atop[...]
    loads[2].wait()

    pending = []
    for layer in range(LAYERS):
        last = layer == LAYERS - 1
        base = NODES * layer
        hb = 6 + 12 * layer

        c0 = coefficients([w2[layer, 0, 0], w2[layer, 0, 1]])

        def act0(e, carry):
            valid = ((e >= 2) | has_up) & ((e < Rm + 2) | has_dn)
            coarse = nt[layer, e // 2].astype(F32) * c0[1]
            for p in range(Pm):
                activate(e, p, nm[layer, e, p].astype(F32) * c0[0] + coarse, valid)
            return carry

        lax.fori_loop(0, Rm + 4, act0, 0)
        depthwise(layer, 0, Rm + 2, Pm)
        t, s = pointwise(layer, 0, Rm + 2, Pm, Rm + 2, raw_d, 1)
        copies = stats_begin(base, t, s)
        if layer == 0:
            loads[3].wait()
            for m in first[4:]:
                arrive(*m)

            def order_fine(e, carry):
                y = jnp.dot(perm_f[0], afine[e], preferred_element_type=F32).astype(BF16)
                for p in range(Pf):
                    nf[0, e, p] = y[p * J : (p + 1) * J]
                return carry

            lax.fori_loop(0, Rf + 2, order_fine, 0)
        second = stats_middle(base, copies)
        sd = stats_end(base, second, layer, 0, float(images * nr * Rm * Wm))

        for m in pending:
            arrive(*m)
        pending = []
        c1 = coefficients([w2[layer, 1, 0], w2[layer, 1, 1]])

        def norm_d(e, carry):
            for p in range(Pm):
                raw_d[e, p] = rounded(normal(raw_d[e, p], sd))
            return carry

        lax.fori_loop(0, Rm + 2, norm_d, 0)

        def act1(e, carry):
            valid = ((e >= 1) | has_up) & ((e < Rf + 1) | has_dn)
            for p in range(Pf):
                down = raw_d[(e + 1) // 2, p // 2] * c1[1]
                activate(e, p, nf[layer, e, p].astype(F32) * c1[0] + down, valid)
            return carry

        lax.fori_loop(0, Rf + 2, act1, 0)
        depthwise(layer, 1, Rf, Pf)
        t, s = pointwise(layer, 1, Rf, Pf, 2, raw_f, 0)
        copies = stats_begin(base + 1, t, s)

        def pool_cols_f(r, carry):
            for q in range(Pm):
                cpf[r, q] = column_pool(raw_f, r, q, Pf)
            return carry

        lax.fori_loop(0, Rf, pool_cols_f, 0)
        up_f[0] = cpf[0]
        up_f[1] = jnp.maximum(jnp.maximum(cpf[0], cpf[1]), cpf[2])
        dn_f[...] = jnp.maximum(cpf[Rf - 2], cpf[Rf - 1])
        edge = [
            (hb, up_f, rup_f.at[layer], True),
            (hb + 1, dn_f, rdn_f.at[layer], False),
        ]
        for m in edge:
            send(*m)

        def pool_rows_f(i, carry):
            pool_f[i + 1] = jnp.maximum(
                jnp.maximum(cpf[2 * i], cpf[2 * i + 1]), cpf[2 * i + 2]
            )
            return carry

        lax.fori_loop(0, Rm - 1, pool_rows_f, 0)
        second = stats_middle(base + 1, copies)
        for m in edge:
            arrive(*m)
        pool_f[0] = jnp.maximum(rdn_f[layer], cpf[0])
        pool_f[Rm] = jnp.maximum(dn_f[...], jnp.where(has_dn, rup_f[layer, 0], -jnp.inf))
        pool_f[Rm + 1] = rup_f[layer, 1]
        sf = stats_end(base + 1, second, layer, 1, float(images * nr * Rf * Wf))

        c2 = coefficients([w3[layer, 0], w3[layer, 1], w3[layer, 2]])

        def act2(e, carry):
            valid = ((e >= 1) | has_up) & ((e < Rm + 1) | has_dn)
            for p in range(Pm):
                half = nm[layer, e + 1, p].astype(F32) * c2[0] + raw_d[e, p] * c2[1]
                half = half + rounded(normal(pool_f[e, p], sf)) * c2[2]
                activate(e, p, half, valid)
            return carry

        lax.fori_loop(0, Rm + 2, act2, 0)
        depthwise(layer, 2, Rm, Pm)
        t, s = pointwise(layer, 2, Rm, Pm, Rm, raw_m, 0)
        copies = stats_begin(base + 2, t, s)

        def pool_cols_m(r, carry):
            cpm[r] = column_pool(raw_m, r, 0, Pm)
            return carry

        lax.fori_loop(0, Rm, pool_cols_m, 0)
        up_m[0] = cpm[0]
        up_m[1] = jnp.maximum(jnp.maximum(cpm[0], cpm[1]), cpm[2])
        dn_m[...] = jnp.maximum(cpm[Rm - 2], cpm[Rm - 1])
        edge = [
            (hb + 2, up_m, rup_m.at[layer], True),
            (hb + 3, dn_m, rdn_m.at[layer], False),
        ]
        for m in edge:
            send(*m)

        def pool_rows_m(i, carry):
            pool_m[i + 1] = jnp.maximum(
                jnp.maximum(cpm[2 * i], cpm[2 * i + 1]), cpm[2 * i + 2]
            )
            return carry

        lax.fori_loop(0, Rt - 1, pool_rows_m, 0)

        if last:

            def finish_f(r, carry):
                for p in range(Pf):
                    sp[pl.ds(p * J, J), :] = normal(raw_f[r, p, pl.ds(0, J), :], sf).astype(BF16)
                of_v[r] = jnp.dot(
                    perm_f[1], sp[pl.ds(0, Wf), :], preferred_element_type=F32
                ).astype(BF16)
                return carry

            lax.fori_loop(0, Rf, finish_f, 0)
            copy_f = pltpu.make_async_copy(of_v, out_f.at[0], outs.at[0])
            copy_f.start()
        else:

            def finish_f(r, carry):
                for p in range(Pf):
                    nf[layer + 1, r + 1, p] = normal(
                        raw_f[r, p, pl.ds(0, J), :], sf
                    ).astype(BF16)
                return carry

            lax.fori_loop(0, Rf, finish_f, 0)
            pending += [
                (hb + 4, nf.at[layer + 1, 1], nf.at[layer + 1, Rf + 1], True),
                (hb + 5, nf.at[layer + 1, Rf], nf.at[layer + 1, 0], False),
            ]
        second = stats_middle(base + 2, copies)
        for m in edge:
            arrive(*m)
        pool_m[0] = jnp.maximum(rdn_m[layer], cpm[0])
        pool_m[Rt] = jnp.maximum(dn_m[...], jnp.where(has_dn, rup_m[layer, 0], -jnp.inf))
        pool_m[Rt + 1] = rup_m[layer, 1]
        sm = stats_end(base + 2, second, layer, 2, float(images * nr * Rm * Wm))

        c3 = coefficients([w2[layer, 2, 0], w2[layer, 2, 1]])

        def act3(e, carry):
            valid = ((e >= 1) | has_up) & ((e < Rt + 1) | has_dn)
            half = nt[layer, e].astype(F32) * c3[0]
            half = half + rounded(normal(pool_m[e], sm)) * c3[1]
            activate(e, 0, half, valid)
            return carry

        lax.fori_loop(0, Rt + 2, act3, 0)
        depthwise(layer, 3, Rt, 1)
        t, s = pointwise(layer, 3, Rt, 1, Rt, raw_t, 0)
        copies = stats_begin(base + 3, t, s)
        if last:

            def finish_m(r, carry):
                for p in range(Pm):
                    sp[pl.ds(p * J, J), :] = normal(raw_m[r, p, pl.ds(0, J), :], sm).astype(BF16)
                om_v[r] = jnp.dot(
                    perm_m[1], sp[pl.ds(0, Wm), :], preferred_element_type=F32
                ).astype(BF16)
                return carry

            lax.fori_loop(0, Rm, finish_m, 0)
            copy_m = pltpu.make_async_copy(om_v, out_m.at[0], outs.at[1])
            copy_m.start()
            second = stats_middle(base + 3, copies)
            st = stats_end(base + 3, second, layer, 3, float(images * nr * Rt * J))
            for r in range(Rt):
                ot_v[r] = normal(raw_t[r, 0], st).astype(BF16)
            copy_t = pltpu.make_async_copy(ot_v, out_t.at[0], outs.at[2])
            copy_t.start()
            for copy in (copy_f, copy_m, copy_t):
                copy.wait()
        else:
            edge = [
                (hb + 6, raw_t.at[0, 0], rup_t.at[layer], True),
                (hb + 7, raw_t.at[Rt - 1, 0], rdn_t.at[layer], False),
            ]
            for m in edge:
                send(*m)

            def finish_m(r, carry):
                for p in range(Pm):
                    nm[layer + 1, r + 2, p] = normal(
                        raw_m[r, p, pl.ds(0, J), :], sm
                    ).astype(BF16)
                return carry

            lax.fori_loop(0, Rm, finish_m, 0)
            rows = [
                (hb + 8, nm.at[layer + 1, pl.ds(2, 2)], nm.at[layer + 1, pl.ds(Rm + 2, 2)], True),
                (hb + 9, nm.at[layer + 1, pl.ds(Rm, 2)], nm.at[layer + 1, pl.ds(0, 2)], False),
            ]
            for m in rows:
                send(*m)
            for m in pending:
                send(*m)
            second = stats_middle(base + 3, copies)
            for m in edge + rows:
                arrive(*m)
            st = stats_end(base + 3, second, layer, 3, float(images * nr * Rt * J))
            nt[layer + 1, 0] = normal(rdn_t[layer], st).astype(BF16)
            for r in range(Rt):
                nt[layer + 1, r + 1] = normal(raw_t[r, 0], st).astype(BF16)
            nt[layer + 1, Rt + 1] = normal(rup_t[layer], st).astype(BF16)


def body(nb, nr, fine, mid, top, w2, w3, dw, pw, gain, bias):
    _, Rf, Wf, C = fine.shape
    _, Rm, Wm, _ = mid.shape
    _, Rt, J, _ = top.shape
    Pf, Pm = Wf // J, Wm // J
    assert fine.shape[0] == 1 and Pf == 4 and Pm == 2 and J % 16 == 0
    assert Rf == 2 * Rm and Rm == 2 * Rt and Rt >= 2
    L = LAYERS
    V = pltpu.VMEM
    scratch = [
        V((Rf + 2, Wf, C), BF16), V((Rm + 4, Wm, C), BF16), V((Rt + 2, J, C), BF16),
        V(pw.shape, BF16),
        V((Rf + 2, Pf, J + 2 * PAD, C), F32), V((Rf * Wf, C), BF16),
        V((Rf, Pf, J + PAD, C), F32), V((Rm + 2, Pm, J, C), F32),
        V((Rm, Pm, J + PAD, C), F32), V((Rt, 1, J, C), F32),
        V((Rf, Pm, J, C), F32), V((Rm, J, C), F32),
        V((Rm + 2, Pm, J, C), F32), V((Rt + 2, J, C), F32),
        V((L, Rf + 2, Pf, J, C), BF16), V((L, Rm + 4, Pm, J, C), BF16), V((L, Rt + 2, J, C), BF16),
        V((2, Pm, J, C), F32), V((Pm, J, C), F32), V((2, J, C), F32), V((J, C), F32),
        V((L, 2, Pm, J, C), F32), V((L, Pm, J, C), F32),
        V((L, 2, J, C), F32), V((L, J, C), F32),
        V((L, J, C), F32), V((L, J, C), F32),
        V((2, Wf, Wf), BF16), V((2, Wm, Wm), BF16),
        V((L * NODES, nb, 2, C), F32), V((L * NODES, nr, 2, C), F32),
        V((Rf, Wf, C), BF16), V((Rm, Wm, C), BF16), V((Rt, J, C), BF16),
        pltpu.SemaphoreType.DMA((L * NODES, nb)), pltpu.SemaphoreType.DMA((L * NODES, nb)),
        pltpu.SemaphoreType.DMA((L * NODES, nr)), pltpu.SemaphoreType.DMA((L * NODES, nr)),
        pltpu.SemaphoreType.DMA((6 + 12 * L,)), pltpu.SemaphoreType.DMA((6 + 12 * L,)),
        pltpu.SemaphoreType.DMA((4,)), pltpu.SemaphoreType.DMA((3,)),
    ]
    hbm = pl.BlockSpec(memory_space=pl.ANY)
    vmem = pl.BlockSpec(memory_space=pltpu.VMEM)
    smem = pl.BlockSpec(memory_space=pltpu.SMEM)
    return tuple(pl.pallas_call(
        functools.partial(kernel, nb, nr),
        out_shape=[jax.ShapeDtypeStruct(a.shape, BF16) for a in (fine, mid, top)],
        in_specs=[hbm, hbm, hbm, smem, smem, vmem, hbm, vmem, vmem],
        out_specs=[hbm, hbm, hbm],
        scratch_shapes=scratch,
        name="bifpn",
        compiler_params=pltpu.CompilerParams(
            collective_id=0, has_side_effects=True, vmem_limit_bytes=56 * 2**20
        ),
    )(fine, mid, top, w2, w3, dw, pw, gain, bias))


def solution(mesh):
    level = P("batch", "rows", None, None)
    return jax.shard_map(
        functools.partial(body, mesh.shape["batch"], mesh.shape["rows"]),
        mesh=mesh,
        in_specs=(level,) * 3 + (P(),) * 6,
        out_specs=(level,) * 3,
        check_vma=False,
    )
```

time: 499 us -> 104 us (0.21)
  blocking collectives: 318 us -> 0 us
  Pallas kernels: 0 us -> 96.2 us
  waiting for transfers between devices: 49.7 us -> 0 us
  other arithmetic: 43 us -> 0 us
  starting transfers between devices: 42.1 us -> 0 us
  local copies, waits for them, and re-layouts: 24.9 us -> 6.64 us
  matrix products: 11.5 us -> 0 us
  between operations: 6.92 us -> 0.66 us
    psum x8 -> x0, blocking collectives: 318 us -> none  [normalize(): lax.psum((jnp.sum(projected, axis=(0, 1, 2)), jnp.sum(projected * project...]
    pallas_call x0 -> x1, Pallas kernels: none -> 96.2 us  [body(): pl.pallas_call(functools.partial(kernel, nb, nr), out_shape=[jax.ShapeDty...]
    ppermute x20 -> x0, waiting for transfers between devices: 49.7 us -> none  [the longest x8 31.3 us: extended_2(): lax.ppermute(lax.slice_in_dim(block, 0, width, axis=dim), axis, backward)]
    ppermute x20 -> x0, starting transfers between devices: 42.1 us -> none  [the longest x8 26.1 us: extended_2(): lax.ppermute(lax.slice_in_dim(block, block.shape[dim] - width, None, axis...]
    convert_element_type x29 -> x0, other arithmetic: 26.9 us -> none  [the longest x8 16.5 us: weighted_join_activate(): return jax.nn.silu(running / weight_sum).astype(jnp.bfloat16)]
    dot_general x8 -> x0, matrix products: 11.5 us -> none  [separable(): jnp.dot(spatial.reshape(-1, spatial.shape[-1]), projection, preferred_ele...]
    mul x4 -> x0, local copies, waits for them, and re-layouts: 9.18 us -> none  [weighted_join_activate(): weights[position] * inputs_list[position].astype(jnp.float32)]
    broadcast_in_dim x8 -> x0, local copies, waits for them, and re-layouts: 5.84 us -> none  [upsample(): return jnp.repeat(jnp.repeat(feature_maps, 2, axis=1), 2, axis=2)]
  transfers between devices with their start and end apart: 20 -> 0, of which waited for: 18 -> 0; matrix products, arithmetic and copies ran while one was open for 1% -> 0% of each run, Pallas kernels for 0% -> 0%
where the time goes in v1:
time: 104 us; the launch traced here: 103 us
  Pallas kernels  96.2 us (92%)
  local copies, waits for them, and re-layouts  6.64 us (6%)
    pallas_call x1, Pallas kernels, body(): pl.pallas_call(functools.partial(kernel, nb, nr), out_shape=[jax.ShapeDty...  96.2 us
    unnamed x9, local copies, waits for them, and re-layouts  6.64 us

profile of v1, /device:TPU:0, one launch (start us, length us, event | category | flops | bytes accessed | tf_op | source)
XLA Modules:
  0.0 103.5 jit_solution(8134836237058558289)
XLA Ops:
  0.6 1.4 %copy.12.w2 = f32[2,3,2]{2,1,0:T(4,128)} copy(f32[2,3,2]{1,2,0:T(2,128)} %param.12) | data formatting | bytes 96 | tf_op args[3]
  2.0 1.5 %copy.13.dw = bf16[2,4,3,3,384]{4,3,2,1,0:T(4,128)(2,1)} copy(bf16[2,4,3,3,384]{4,1,3,2,0:T(4,128)(2,1)} %param.14) | data formatting | bytes 110592 | tf_op args[5]
  3.5 96.2 %bifpn.1 = (bf16[1,8,192,384]{3,2,1,0:T(8,128)(2,1)}, bf16[1,4,96,384]{3,2,1,0:T(8,128)(2,1)}, bf16[1,2,48,384]{3,2,1,0:T(8,128)(2,1)}) custom-call(bf16[1,8,192,384]{3,2,1,0:T(8,128)(2,1)} %fine.1, bf16[1,4,96,384]{3,2,1,0:T(8,128)(2,1)} %mid.1, bf16[1,2,48,384]{3,2,1,0:T(8,128)(2,1)} %top.1, f32[2,3,2]{2,1,0:T(4,128)} %copy.12.w2, f32[2,3]{1,0:T(2,128)} %w3.1, ...), custom_call_target="tpu_custom_call" | custom-call | tf_op jit(solution)/shard_map/bifpn/pallas_call | solution.py:499
  99.6 0.0 copy-start
  99.6 0.0 copy-start.1
  99.7 2.4 %copy.17 = bf16[1,8,192,384]{3,2,1,0:T(8,128)(2,1)} copy(bf16[1,8,192,384]{3,2,1,0:T(8,128)(2,1)} %get-tuple-element.6) | data formatting | bytes 2359296
  102.1 0.0 copy-done
  102.1 0.7 copy.18
  102.8 0.0 copy-done.1
  102.8 0.6 copy.19
Async XLA Ops:
  99.6 2.5 %copy-start = (bf16[1,4,96,384]{3,2,1,0:T(8,128)(2,1)S(1)}, bf16[1,4,96,384]{3,2,1,0:T(8,128)(2,1)}, u32[]{:S(2)}) copy-start(bf16[1,4,96,384]{3,2,1,0:T(8,128)(2,1)} %get-tuple-element.7) | copy-start | bytes 884740
  99.6 3.2 %copy-start.1 = (bf16[1,2,48,384]{3,2,1,0:T(8,128)(2,1)S(1)}, bf16[1,2,48,384]{3,2,1,0:T(8,128)(2,1)}, u32[]{:S(2)}) copy-start(bf16[1,2,48,384]{3,2,1,0:T(8,128)(2,1)} %get-tuple-element.8) | copy-start | bytes 221188

commit v2 on v1

--- a/solution.py
+++ b/solution.py
@@ -36,9 +36,9 @@
     out_f, out_m, out_t,
     afine, amid, atop, pw, act, sp, raw_f, raw_d, raw_m, raw_t,
     cpf, cpm, pool_f, pool_m, nf, nm, nt,
-    up_f, dn_f, up_m, dn_m, rup_f, rdn_f, rup_m, rdn_m, rup_t, rdn_t,
-    perm_f, perm_m, stat_b, stat_r, of_v, om_v, ot_v,
-    sb_s, sb_r, sr_s, sr_r, h_s, h_r, loc, outs,
+    up_f, dn_f, up_m, dn_m, rup_f, rdn_f, rup_m, rdn_m, rup_t, rdn_t, edge_t,
+    perm_f, perm_m, stat_b,
+    sb_s, sb_r, h_s, h_r, loc,
 ):
     b_me = lax.axis_index("batch")
     r_me = lax.axis_index("rows")
@@ -62,13 +62,11 @@
         copy.start()
 
     barrier = pltpu.get_barrier_semaphore()
-    for d in range(1, nb):
+    for d in range(1, nb * nr):
         pl.semaphore_signal(
-            barrier, inc=1, device_id={"batch": lax.rem(b_me + d, nb)}, device_id_type=MESH
-        )
-    for d in range(1, nr):
-        pl.semaphore_signal(
-            barrier, inc=1, device_id={"rows": lax.rem(r_me + d, nr)}, device_id_type=MESH
+            barrier, inc=1,
+            device_id={"batch": lax.rem(b_me + d // nr, nb), "rows": lax.rem(r_me + d % nr, nr)},
+            device_id_type=MESH,
         )
 
     def message(k, src, dst, up):
@@ -91,39 +89,28 @@
         def _():
             message(k, src, dst, up).wait_send()
 
-    def spread_copies(store, sends, recvs, node, me, count, axis):
-        return [
-            pltpu.make_async_remote_copy(
-                src_ref=store.at[node, me], dst_ref=store.at[node, me],
-                send_sem=sends.at[node, d], recv_sem=recvs.at[node, d],
-                device_id={axis: lax.rem(me + d, count)}, device_id_type=MESH,
-            )
-            for d in range(1, count)
-        ]
-
     def stats_begin(node, total, square):
-        stat_b[node, b_me, 0:1, :] = total
-        stat_b[node, b_me, 1:2, :] = square
-        copies = spread_copies(stat_b, sb_s, sb_r, node, b_me, nb, "batch")
-        for copy in copies:
-            copy.start()
+        me = b_me * nr + r_me
+        stat_b[node, me, 0:1, :] = total
+        stat_b[node, me, 1:2, :] = square
+        copies = []
+        for db in range(nb):
+            for dr in range(nr):
+                d = db * nr + dr
+                if d:
+                    copies.append(pltpu.make_async_remote_copy(
+                        src_ref=stat_b.at[node, me], dst_ref=stat_b.at[node, me],
+                        send_sem=sb_s.at[d], recv_sem=sb_r.at[node, d],
+                        device_id={"batch": lax.rem(b_me + db, nb), "rows": lax.rem(r_me + dr, nr)},
+                        device_id_type=MESH,
+                    ))
+                    copies[-1].start()
         return copies
-
-    def stats_middle(node, copies):
-        for copy in copies:
-            copy.wait_recv()
-        stat_r[node, r_me] = jnp.sum(stat_b[node], axis=0)
-        second = spread_copies(stat_r, sr_s, sr_r, node, r_me, nr, "rows")
-        for copy in second:
-            copy.start()
-        for copy in copies:
-            copy.wait_send()
-        return second
 
     def stats_end(node, copies, layer, which, count):
         for copy in copies:
             copy.wait_recv()
-        sums = jnp.sum(stat_r[node], axis=0)
+        sums = jnp.sum(stat_b[node], axis=0)
         for copy in copies:
             copy.wait_send()
         center = sums[0:1] / count
@@ -146,11 +133,11 @@
         a = rounded(half + half * jnp.tanh(half))
         act[row, p, pl.ds(PAD, J), :] = jnp.where(valid, a, 0.0)
 
-    def depthwise(layer, which, rows, phases):
+    def depthwise(layer, which, rows, phases, body_only=False):
         taps = []
         for i in range(3):
-            k = dw[layer, which, i].astype(F32)
-            taps.append([k[j : j + 1] for j in range(3)])
+            rows_of = [dw[layer, i, j].astype(F32) for j in range(3)]
+            taps.append([k[which : which + 1] for k in rows_of])
 
         def body(r, carry):
             for p in range(phases):
@@ -167,9 +154,27 @@
                 sp[pl.ds(pl.multiple_of((r * phases + p) * J, J), J), :] = total.astype(BF16)
             return carry
 
+        if body_only:
+            return body
         lax.fori_loop(0, rows, body, 0)
 
-    def pointwise(layer, which, rows, phases, chunk, dst, skip):
+    def fused(layer, which, rows, phases, chunk, dst):
+        one_row = depthwise(layer, which, rows, phases, True)
+        product = pointwise(layer, which, rows, phases, chunk, dst, 0, True)
+        zero = jnp.zeros((1, C), F32)
+        for r in range(chunk):
+            one_row(r, 0)
+
+        def step(i, carry):
+            carry = product(i * chunk, carry)
+            for r in range(chunk):
+                one_row((i + 1) * chunk + r, 0)
+            return carry
+
+        carry = lax.fori_loop(0, rows // chunk - 1, step, (zero, zero))
+        return product(rows - chunk, carry)
+
+    def pointwise(layer, which, rows, phases, chunk, dst, skip, body_only=False):
         width = phases * J
 
         def one(first, carry):
@@ -187,6 +192,8 @@
                 carry[1] + jnp.sum(kept * kept, axis=0, keepdims=True),
             )
 
+        if body_only:
+            return one
         zero = jnp.zeros((1, C), F32)
         if chunk == rows:
             return one(0, (zero, zero))
@@ -203,7 +210,7 @@
     raw_f[:, :, J : J + PAD, :] = jnp.full((Rf, Pf, PAD, C), -jnp.inf, F32)
     raw_m[:, :, J : J + PAD, :] = jnp.full((Rm, Pm, PAD, C), -jnp.inf, F32)
 
-    pl.semaphore_wait(barrier, nb + nr - 2)
+    pl.semaphore_wait(barrier, nb * nr - 1)
     first = [
         (0, mid.at[0, pl.ds(0, 2)], amid.at[pl.ds(Rm + 2, 2)], True),
         (1, mid.at[0, pl.ds(Rm - 2, 2)], amid.at[pl.ds(0, 2)], False),
@@ -239,7 +246,7 @@
         base = NODES * layer
         hb = 6 + 12 * layer
 
-        c0 = coefficients([w2[layer, 0, 0], w2[layer, 0, 1]])
+        c0 = coefficients([w2[layer, 0, 0], w2[layer, 1, 0]])
 
         def act0(e, carry):
             valid = ((e >= 2) | has_up) & ((e < Rm + 2) | has_dn)
@@ -264,13 +271,12 @@
                 return carry
 
             lax.fori_loop(0, Rf + 2, order_fine, 0)
-        second = stats_middle(base, copies)
-        sd = stats_end(base, second, layer, 0, float(images * nr * Rm * Wm))
+        sd = stats_end(base, copies, layer, 0, float(images * nr * Rm * Wm))
 
         for m in pending:
             arrive(*m)
         pending = []
-        c1 = coefficients([w2[layer, 1, 0], w2[layer, 1, 1]])
+        c1 = coefficients([w2[layer, 0, 1], w2[layer, 1, 1]])
 
         def norm_d(e, carry):
             for p in range(Pm):
@@ -287,8 +293,7 @@
             return carry
 
         lax.fori_loop(0, Rf + 2, act1, 0)
-        depthwise(layer, 1, Rf, Pf)
-        t, s = pointwise(layer, 1, Rf, Pf, 2, raw_f, 0)
+        t, s = fused(layer, 1, Rf, Pf, 2, raw_f)
         copies = stats_begin(base + 1, t, s)
 
         def pool_cols_f(r, carry):
@@ -297,9 +302,11 @@
             return carry
 
         lax.fori_loop(0, Rf, pool_cols_f, 0)
-        up_f[0] = cpf[0]
-        up_f[1] = jnp.maximum(jnp.maximum(cpf[0], cpf[1]), cpf[2])
-        dn_f[...] = jnp.maximum(cpf[Rf - 2], cpf[Rf - 1])
+        up_f[0] = cpf[0].astype(BF16)
+        up_f[1] = jnp.maximum(jnp.maximum(cpf[0], cpf[1]), cpf[2]).astype(BF16)
+        bottom = jnp.maximum(cpf[Rf - 2], cpf[Rf - 1])
+        dn_f[...] = bottom.astype(BF16)
+        pool_f[Rm] = bottom
         edge = [
             (hb, up_f, rup_f.at[layer], True),
             (hb + 1, dn_f, rdn_f.at[layer], False),
@@ -314,13 +321,14 @@
             return carry
 
         lax.fori_loop(0, Rm - 1, pool_rows_f, 0)
-        second = stats_middle(base + 1, copies)
         for m in edge:
             arrive(*m)
-        pool_f[0] = jnp.maximum(rdn_f[layer], cpf[0])
-        pool_f[Rm] = jnp.maximum(dn_f[...], jnp.where(has_dn, rup_f[layer, 0], -jnp.inf))
-        pool_f[Rm + 1] = rup_f[layer, 1]
-        sf = stats_end(base + 1, second, layer, 1, float(images * nr * Rf * Wf))
+        pool_f[0] = jnp.maximum(rdn_f[layer].astype(F32), cpf[0])
+        pool_f[Rm] = jnp.maximum(
+            pool_f[Rm], jnp.where(has_dn, rup_f[layer, 0].astype(F32), -jnp.inf)
+        )
+        pool_f[Rm + 1] = rup_f[layer, 1].astype(F32)
+        sf = stats_end(base + 1, copies, layer, 1, float(images * nr * Rf * Wf))
 
         c2 = coefficients([w3[layer, 0], w3[layer, 1], w3[layer, 2]])
 
@@ -342,9 +350,11 @@
             return carry
 
         lax.fori_loop(0, Rm, pool_cols_m, 0)
-        up_m[0] = cpm[0]
-        up_m[1] = jnp.maximum(jnp.maximum(cpm[0], cpm[1]), cpm[2])
-        dn_m[...] = jnp.maximum(cpm[Rm - 2], cpm[Rm - 1])
+        up_m[0] = cpm[0].astype(BF16)
+        up_m[1] = jnp.maximum(jnp.maximum(cpm[0], cpm[1]), cpm[2]).astype(BF16)
+        bottom = jnp.maximum(cpm[Rm - 2], cpm[Rm - 1])
+        dn_m[...] = bottom.astype(BF16)
+        pool_m[Rt] = bottom
         edge = [
             (hb + 2, up_m, rup_m.at[layer], True),
             (hb + 3, dn_m, rdn_m.at[layer], False),
@@ -365,14 +375,12 @@
             def finish_f(r, carry):
                 for p in range(Pf):
                     sp[pl.ds(p * J, J), :] = normal(raw_f[r, p, pl.ds(0, J), :], sf).astype(BF16)
-                of_v[r] = jnp.dot(
+                out_f[0, r] = jnp.dot(
                     perm_f[1], sp[pl.ds(0, Wf), :], preferred_element_type=F32
                 ).astype(BF16)
                 return carry
 
             lax.fori_loop(0, Rf, finish_f, 0)
-            copy_f = pltpu.make_async_copy(of_v, out_f.at[0], outs.at[0])
-            copy_f.start()
         else:
 
             def finish_f(r, carry):
@@ -387,15 +395,16 @@
                 (hb + 4, nf.at[layer + 1, 1], nf.at[layer + 1, Rf + 1], True),
                 (hb + 5, nf.at[layer + 1, Rf], nf.at[layer + 1, 0], False),
             ]
-        second = stats_middle(base + 2, copies)
         for m in edge:
             arrive(*m)
-        pool_m[0] = jnp.maximum(rdn_m[layer], cpm[0])
-        pool_m[Rt] = jnp.maximum(dn_m[...], jnp.where(has_dn, rup_m[layer, 0], -jnp.inf))
-        pool_m[Rt + 1] = rup_m[layer, 1]
-        sm = stats_end(base + 2, second, layer, 2, float(images * nr * Rm * Wm))
-
-        c3 = coefficients([w2[layer, 2, 0], w2[layer, 2, 1]])
+        pool_m[0] = jnp.maximum(rdn_m[layer].astype(F32), cpm[0])
+        pool_m[Rt] = jnp.maximum(
+            pool_m[Rt], jnp.where(has_dn, rup_m[layer, 0].astype(F32), -jnp.inf)
+        )
+        pool_m[Rt + 1] = rup_m[layer, 1].astype(F32)
+        sm = stats_end(base + 2, copies, layer, 2, float(images * nr * Rm * Wm))
+
+        c3 = coefficients([w2[layer, 0, 2], w2[layer, 1, 2]])
 
         def act3(e, carry):
             valid = ((e >= 1) | has_up) & ((e < Rt + 1) | has_dn)
@@ -413,26 +422,21 @@
             def finish_m(r, carry):
                 for p in range(Pm):
                     sp[pl.ds(p * J, J), :] = normal(raw_m[r, p, pl.ds(0, J), :], sm).astype(BF16)
-                om_v[r] = jnp.dot(
+                out_m[0, r] = jnp.dot(
                     perm_m[1], sp[pl.ds(0, Wm), :], preferred_element_type=F32
                 ).astype(BF16)
                 return carry
 
             lax.fori_loop(0, Rm, finish_m, 0)
-            copy_m = pltpu.make_async_copy(om_v, out_m.at[0], outs.at[1])
-            copy_m.start()
-            second = stats_middle(base + 3, copies)
-            st = stats_end(base + 3, second, layer, 3, float(images * nr * Rt * J))
+            st = stats_end(base + 3, copies, layer, 3, float(images * nr * Rt * J))
             for r in range(Rt):
-                ot_v[r] = normal(raw_t[r, 0], st).astype(BF16)
-            copy_t = pltpu.make_async_copy(ot_v, out_t.at[0], outs.at[2])
-            copy_t.start()
-            for copy in (copy_f, copy_m, copy_t):
-                copy.wait()
+                out_t[0, r] = normal(raw_t[r, 0], st).astype(BF16)
         else:
+            edge_t[0] = raw_t[0, 0].astype(BF16)
+            edge_t[1] = raw_t[Rt - 1, 0].astype(BF16)
             edge = [
-                (hb + 6, raw_t.at[0, 0], rup_t.at[layer], True),
-                (hb + 7, raw_t.at[Rt - 1, 0], rdn_t.at[layer], False),
+                (hb + 6, edge_t.at[0], rup_t.at[layer], True),
+                (hb + 7, edge_t.at[1], rdn_t.at[layer], False),
             ]
             for m in edge:
                 send(*m)
@@ -453,14 +457,13 @@
                 send(*m)
             for m in pending:
                 send(*m)
-            second = stats_middle(base + 3, copies)
             for m in edge + rows:
                 arrive(*m)
-            st = stats_end(base + 3, second, layer, 3, float(images * nr * Rt * J))
-            nt[layer + 1, 0] = normal(rdn_t[layer], st).astype(BF16)
+            st = stats_end(base + 3, copies, layer, 3, float(images * nr * Rt * J))
+            nt[layer + 1, 0] = normal(rdn_t[layer].astype(F32), st).astype(BF16)
             for r in range(Rt):
                 nt[layer + 1, r + 1] = normal(raw_t[r, 0], st).astype(BF16)
-            nt[layer + 1, Rt + 1] = normal(rup_t[layer], st).astype(BF16)
+            nt[layer + 1, Rt + 1] = normal(rup_t[layer].astype(F32), st).astype(BF16)
 
 
 def body(nb, nr, fine, mid, top, w2, w3, dw, pw, gain, bias):
@@ -481,32 +484,30 @@
         V((Rf, Pm, J, C), F32), V((Rm, J, C), F32),
         V((Rm + 2, Pm, J, C), F32), V((Rt + 2, J, C), F32),
         V((L, Rf + 2, Pf, J, C), BF16), V((L, Rm + 4, Pm, J, C), BF16), V((L, Rt + 2, J, C), BF16),
-        V((2, Pm, J, C), F32), V((Pm, J, C), F32), V((2, J, C), F32), V((J, C), F32),
-        V((L, 2, Pm, J, C), F32), V((L, Pm, J, C), F32),
-        V((L, 2, J, C), F32), V((L, J, C), F32),
-        V((L, J, C), F32), V((L, J, C), F32),
+        V((2, Pm, J, C), BF16), V((Pm, J, C), BF16), V((2, J, C), BF16), V((J, C), BF16),
+        V((L, 2, Pm, J, C), BF16), V((L, Pm, J, C), BF16),
+        V((L, 2, J, C), BF16), V((L, J, C), BF16),
+        V((L, J, C), BF16), V((L, J, C), BF16), V((2, J, C), BF16),
         V((2, Wf, Wf), BF16), V((2, Wm, Wm), BF16),
-        V((L * NODES, nb, 2, C), F32), V((L * NODES, nr, 2, C), F32),
-        V((Rf, Wf, C), BF16), V((Rm, Wm, C), BF16), V((Rt, J, C), BF16),
-        pltpu.SemaphoreType.DMA((L * NODES, nb)), pltpu.SemaphoreType.DMA((L * NODES, nb)),
-        pltpu.SemaphoreType.DMA((L * NODES, nr)), pltpu.SemaphoreType.DMA((L * NODES, nr)),
+        V((L * NODES, nb * nr, 2, C), F32),
+        pltpu.SemaphoreType.DMA((nb * nr,)), pltpu.SemaphoreType.DMA((L * NODES, nb * nr)),
         pltpu.SemaphoreType.DMA((6 + 12 * L,)), pltpu.SemaphoreType.DMA((6 + 12 * L,)),
-        pltpu.SemaphoreType.DMA((4,)), pltpu.SemaphoreType.DMA((3,)),
+        pltpu.SemaphoreType.DMA((4,)),
     ]
     hbm = pl.BlockSpec(memory_space=pl.ANY)
     vmem = pl.BlockSpec(memory_space=pltpu.VMEM)
     smem = pl.BlockSpec(memory_space=pltpu.SMEM)
     return tuple(pl.pallas_call(
         functools.partial(kernel, nb, nr),
-        out_shape=[jax.ShapeDtypeStruct(a.shape, BF16) for a in (fine, mid, top)],
+        out_shape=[pltpu.VMEM(a.shape, BF16) for a in (fine, mid, top)],
         in_specs=[hbm, hbm, hbm, smem, smem, vmem, hbm, vmem, vmem],
-        out_specs=[hbm, hbm, hbm],
+        out_specs=[vmem, vmem, vmem],
         scratch_shapes=scratch,
         name="bifpn",
         compiler_params=pltpu.CompilerParams(
             collective_id=0, has_side_effects=True, vmem_limit_bytes=56 * 2**20
         ),
-    )(fine, mid, top, w2, w3, dw, pw, gain, bias))
+    )(fine, mid, top, jnp.swapaxes(w2, 1, 2), w3, jnp.transpose(dw, (0, 2, 3, 1, 4)), pw, gain, bias))
 
 
 def solution(mesh):

time: 104 us -> 85.7 us (0.82)
  Pallas kernels: 96.2 us -> 82.5 us
  local copies, waits for them, and re-layouts: 6.64 us -> 2.36 us
    pallas_call x1, Pallas kernels: 96.2 us -> 82.5 us  [body(): pl.pallas_call(functools.partial(kernel, nb, nr), out_shape=[pltpu.VMEM(a...]
    unnamed x9 -> x3, local copies, waits for them, and re-layouts: 6.64 us -> 2.36 us
where the time goes in v2:
time: 85.7 us; the launch traced here: 85.5 us
  Pallas kernels  82.5 us (96%)
  local copies, waits for them, and re-layouts  2.36 us (3%)
    pallas_call x1, Pallas kernels, body(): pl.pallas_call(functools.partial(kernel, nb, nr), out_shape=[pltpu.VMEM(a...  82.5 us
    unnamed x3, local copies, waits for them, and re-layouts  2.36 us

profile of v2, /device:TPU:0, one launch (start us, length us, event | category | flops | bytes accessed | tf_op | source)
XLA Modules:
  0.0 85.5 jit_solution(13528119608679711925)
XLA Ops:
  0.6 82.5 %bifpn.1 = (bf16[1,8,192,384]{3,2,1,0:T(8,128)(2,1)S(1)}, bf16[1,4,96,384]{3,2,1,0:T(8,128)(2,1)S(1)}, bf16[1,2,48,384]{3,2,1,0:T(8,128)(2,1)S(1)}) custom-call(bf16[1,8,192,384]{3,2,1,0:T(8,128)(2,1)} %fine.1, bf16[1,4,96,384]{3,2,1,0:T(8,128)(2,1)} %mid.1, bf16[1,2,48,384]{3,2,1,0:T(8,128)(2,1)} %top.1, f32[2,2,3]{2,1,0:T(2,128)} %bitcast.3, f32[2,3]{1,0:T(2,128)} %w3.1, ...), custom_call_target="tpu_custom_call" | custom-call | tf_op jit(solution)/shard_map/bifpn/pallas_call | solution.py:500
  83.2 1.0 %copy.15 = bf16[1,8,192,384]{3,2,1,0:T(8,128)(2,1)} copy(bf16[1,8,192,384]{3,2,1,0:T(8,128)(2,1)S(1)} %get-tuple-element.3) | data formatting | bytes 2359296
  84.2 0.6 copy.17
  84.8 0.7 copy.16
